TPU v7x, 32 devices: a whole 2x2x4 slice. The times are simulated.
32 devices in a mesh: alpha: 4 (over z), beta: 4 (over y, core), task: 2 (over x).
Axes of the slice: x: 2, y: 2, z: 4, core: 2. Of those that a mesh axis runs over, the one named last changes fastest.
Arguments:
- vector: float32 [1024, 4096], P('alpha', 'beta'), may hold values from -6 to 6
- op_alpha: float32 [2, 1024, 1024], P('task', 'alpha'), may hold values from -2 to 2, as said below
- op_beta: float32 [2, 4096, 4096], P('task', 'beta'), may hold values from -2 to 2, as said below
- op_weight: float32 [2], replicated, may hold values from 0.5 to 2
- alpha_string: int32 [1024], P('alpha'), may hold values from 0 to 65535
- beta_string: int32 [4096], P('beta'), may hold values from 0 to 65535
- alpha_energy: float32 [65536], replicated, may hold values from -4 to 4
- beta_energy: float32 [65536], replicated, may hold values from -4 to 4
Outputs:
- sigma: float32 [1024, 4096], P('alpha', ('beta', 'task'))
Inputs may be any that keep to these rules, and one draw needn't show every extreme that they name: Every op_alpha[k] is a symmetric matrix. Every op_beta[k] is a symmetric matrix.
All inputs are finite; a program needn't handle non-finite values.
Results may differ from a plain program's by a relative error of at most 0.0001.
Values sent between devices are 32-bit elements; how exact they have to be, the bound alone decides.
A program may use at most 128 MiB of HBM per device.

v0:
```python
import jax
import jax.numpy as jnp
from jax import lax
from jax.sharding import PartitionSpec as P


def on_device(
    vector, op_alpha, op_beta, op_weight, alpha_string, beta_string, alpha_energy, beta_energy
):
    highest = lax.Precision.HIGHEST
    alpha_rows = op_alpha[0]
    beta_rows = op_beta[0]

    def alpha_product(block):
        return jnp.dot(
            alpha_rows,
            lax.all_gather(block, "alpha", axis=0, tiled=True),
            precision=highest,
            preferred_element_type=jnp.float32,
        )

    def beta_product(block):
        partial_value = jnp.dot(
            block, beta_rows, precision=highest, preferred_element_type=jnp.float32
        )
        return lax.psum_scatter(partial_value, "beta", scatter_dimension=1, tiled=True)

    def apply_operator(block):
        return alpha_product(block) + beta_product(block)

    inter = apply_operator(vector)
    second = apply_operator(inter)
    task_index = lax.axis_index("task")
    coefficient = op_weight[task_index]
    summed = lax.psum_scatter(0.5 * coefficient * second, "task", scatter_dimension=1, tiled=True)
    width = summed.shape[1]
    column_start = task_index * width
    own_strings = lax.dynamic_slice_in_dim(beta_string, column_start, width, 0)
    own_vector = lax.dynamic_slice_in_dim(vector, column_start, width, 1)
    diag = alpha_energy[alpha_string][:, None] + beta_energy[own_strings][None, :]
    return summed + diag * own_vector


def solution(mesh):
    return jax.shard_map(
        on_device,
        mesh=mesh,
        in_specs=(
            P("alpha", "beta"),
            P("task", "alpha", None),
            P("task", "beta", None),
            P(),
            P("alpha"),
            P("beta"),
            P(),
            P(),
        ),
        out_specs=P("alpha", ("beta", "task")),
        check_vma=False,
    )
```

profile of v0, /device:TPU:0, one launch (start us, length us, event | category | flops | bytes accessed | tf_op | source)
XLA Modules:
  0.0 218.5 jit_solution(7641866637916102209)
XLA Ops:
  7.4 0.7 all-gather.3.cloned.1.call-update
  8.1 0.0 reduce-scatter.4.cloned.1.call-start
  8.1 18.3 %fusion.2 = f32[256,4096]{1,0:T(8,128)} fusion(f32[256,1024]{1,0:T(8,128)} %param.8, f32[1,1024,4096]{2,1,0:T(8,128)} %param.10), kind=kOutput, calls=%fused_computation.4 | convolution fusion | flops 12884901888 | bytes 22020096 | tf_op jit(solution)/shard_map/dot_general | solution.py:23
  26.5 0.0 reduce-scatter.4.cloned.1.call-update
  26.5 0.0 all-gather.5.cloned.1.call-start
  26.5 66.7 %all-gather.3.cloned.1.call-done = f32[1024,1024]{1,0:T(8,128)} async-done(((f32[256,1024]{1,0:T(8,128)}), f32[1024,1024]{1,0:T(8,128)}) %all-gather.3.cloned.1.call-update) | async-done | bytes 4194320 | tf_op jit(solution)/shard_map/all_gather | solution.py:17
  93.3 7.2 %convolution_add_fusion = f32[256,1024]{1,0:T(8,128)} fusion(f32[256,1024]{1,0:T(8,128)} %reduce-scatter.4.cloned.1.call-done, f32[1024,1024]{1,0:T(8,128)} %all-gather.3.cloned.1.call-done, f32[1,256,1024]{2,1,0:T(8,128)S(1)} %copy-done), kind=kOutput, calls=%fused_computation.9 | convolution fusion | flops 3221487616 | bytes 7340032 | tf_op jit(solution)/shard_map/dot_general | solution.py:15
  100.5 0.0 all-gather.5.cloned.1.call-update
  100.5 0.2 reduce-scatter.6.cloned.1.call-start
  100.8 30.2 %fusion = f32[256,4096]{0,1:T(8,128)} fusion(f32[256,1024]{1,0:T(8,128)} %convolution_add_fusion, f32[1,1024,4096]{2,1,0:T(8,128)} %param.10), kind=kOutput, calls=%fused_computation.2 | convolution fusion | flops 12884901888 | bytes 22020096 | tf_op jit(solution)/shard_map/dot_general | solution.py:23
  131.0 0.0 reduce-scatter.6.cloned.1.call-update
  131.0 0.3 reduce-scatter.8.cloned.1.call-start
  131.3 0.4 copy-done.6
  131.6 0.6 dynamic_slice.9
  132.9 47.0 %all-gather.5.cloned.1.call-done = f32[1024,1024]{1,0:T(8,128)} async-done(((f32[256,1024]{1,0:T(8,128)}), f32[1024,1024]{1,0:T(8,128)}) %all-gather.5.cloned.1.call-update) | async-done | bytes 4194320 | tf_op jit(solution)/shard_map/all_gather | solution.py:17
  179.9 10.2 %fusion.5 = f32[256,1024]{0,1:T(8,128)} fusion(f32[256,1024]{0,1:T(8,128)} %reduce-scatter.6.cloned.1.call-done, f32[1024,1024]{1,0:T(8,128)} %all-gather.5.cloned.1.call-done, f32[1,256,1024]{2,1,0:T(8,128)S(1)} %copy-done, f32[]{:T(128)} %bitcast), kind=kOutput, calls=%fused_computation.8 | convolution fusion | flops 3221749760 | bytes 7340036 | tf_op jit(solution)/shard_map/dot_general | solution.py:15
  190.1 0.0 reduce-scatter.8.cloned.1.call-update
  190.2 0.2 copy.16
  190.4 0.1 compare_select_fusion
  190.5 3.1 %gather_fusion.1 = f32[512]{0:T(512)S(1)} fusion(f32[65536]{0:T(1024)S(1)} %copy-done.1, s32[1024]{0:T(1024)S(1)} %pad_clamp_fusion), kind=kCustom, calls=%fused_computation.1 | custom fusion | bytes 6144 | tf_op jit(solution)/shard_map/gather | solution.py:40
  193.7 1.7 gather_fusion
  195.4 13.7 %reduce-scatter.8.cloned.1.call-done = f32[256,512]{0,1:T(8,128)} async-done(((f32[256,1024]{0,1:T(8,128)}), f32[256,512]{0,1:T(8,128)}) %reduce-scatter.8.cloned.1.call-update) | async-done | bytes 524304 | tf_op jit(solution)/shard_map/reduce_scatter | solution.py:35
  209.2 1.2 multiply_add_fusion
  210.3 1.0 copy.14
  (20 shorter events, 0.1 us)
Async XLA Ops:
  7.4 85.9 %copy-start = (f32[1,256,1024]{2,1,0:T(8,128)S(1)}, f32[1,256,1024]{2,1,0:T(8,128)}, u32[]{:S(2)}) copy-start(f32[1,256,1024]{2,1,0:T(8,128)} %param.9) | copy-start | bytes 3145732
  7.4 85.9 %all-gather.3.cloned.1.call-start = ((), (), s32[]{:S(2)}) async-start(), calls=%async_computation.3 | async-start | bytes 5242880 | tf_op jit(solution)/shard_map/all_gather | solution.py:17
  8.1 85.2 %reduce-scatter.4.cloned.1.call-start = ((), (), s32[]{:S(2)}) async-start(), calls=%async_computation.4 | async-start | bytes 5242880 | tf_op jit(solution)/shard_map/reduce_scatter | solution.py:26
  26.5 153.4 %all-gather.5.cloned.1.call-start = ((), (), s32[]{:S(2)}) async-start(), calls=%async_computation.5 | async-start | bytes 5242880 | tf_op jit(solution)/shard_map/all_gather | solution.py:17
  100.5 79.4 %reduce-scatter.6.cloned.1.call-start = ((), (), s32[]{:S(2)}) async-start(), calls=%async_computation.6 | async-start | bytes 5242880 | tf_op jit(solution)/shard_map/reduce_scatter | solution.py:26
  131.0 0.7 copy-start.6
  131.0 78.1 %reduce-scatter.8.cloned.1.call-start = ((), (), s32[]{:S(2)}) async-start(), calls=%async_computation.7 | async-start | bytes 1572864 | tf_op jit(solution)/shard_map/reduce_scatter | solution.py:35
  179.9 10.3 %copy-start.2 = (f32[256,1024]{1,0:T(8,128)S(1)}, f32[256,1024]{1,0:T(8,128)}, u32[]{:S(2)}) copy-start(f32[256,1024]{1,0:T(8,128)} %param.8) | copy-start | bytes 3145732
  179.9 10.5 %copy-start.4 = (s32[1024]{0:T(1024)S(1)}, s32[1024]{0:T(1024)}, u32[]{:S(2)}) copy-start(s32[1024]{0:T(1024)} %param.13) | copy-start | bytes 12292
  179.9 10.6 %copy-start.1 = (f32[65536]{0:T(1024)S(1)}, f32[65536]{0:T(1024)}, u32[]{:S(2)}) copy-start(f32[65536]{0:T(1024)} %param.15) | copy-start | bytes 786436
  190.1 3.6 %copy-start.5 = (s32[256]{0:T(256)S(1)}, s32[256]{0:T(256)}, u32[]{:S(2)}) copy-start(s32[256]{0:T(256)} %param.12) | copy-start | bytes 3076
  190.1 3.6 %copy-start.3 = (f32[65536]{0:T(1024)S(1)}, f32[65536]{0:T(1024)}, u32[]{:S(2)}) copy-start(f32[65536]{0:T(1024)} %param.14) | copy-start | bytes 786436
Sparse Core Ops, SparseCore 0:
  9.7 83.4 all-gather.2
  100.6 79.1 all-gather.4
  190.3 18.8 reduce-scatter.7
Sparse Core Ops, SparseCore 1:
  26.6 47.0 reduce-scatter.3
  131.1 42.9 reduce-scatter.5
where the time goes:
time: 219 us; the launch traced here: 218 us
  waiting for transfers between devices  128 us (58%)
  matrix products  66 us (30%)
  between operations  15.3 us (7%)
  local copies, waits for them, and re-layouts  7.06 us (3%)
    all_gather x2, waiting for transfers between devices, alpha_product(): lax.all_gather(block, 'alpha', axis=0, tiled=True)  114 us
    dot_general x2, matrix products, beta_product(): jnp.dot(block, beta_rows, precision=highest, preferred_element_type=jnp.f...  48.5 us
    dot_general x2, matrix products, alpha_product(): jnp.dot(alpha_rows, lax.all_gather(block, 'alpha', axis=0, tiled=True), p...  17.4 us
    reduce_scatter x1, waiting for transfers between devices, on_device(): lax.psum_scatter(0.5 * coefficient * second, 'task', scatter_dimension=1,...  13.7 us
  transfers between devices with their start and end apart: 5, of which 3 were waited for; matrix products, arithmetic and copies ran while one was open for 25% of the time, Pallas kernels for 0%

commit v1 on v0

v1 whole, which is shorter than its diff:
```python
import functools

import jax
import jax.numpy as jnp
from jax import lax
from jax.experimental import pallas as pl
from jax.experimental.pallas import tpu as pltpu
from jax.sharding import PartitionSpec as P

MESH = pl.DeviceIdType.MESH
F32 = jnp.float32
BF16 = jnp.bfloat16
TILE = 256
STRIP = 128
VMEM_BUDGET = 56 * 1024 * 1024


def halves(x):
    high = x.astype(BF16)
    return high, (x - high.astype(F32)).astype(BF16)


def product(stack, right_high, right_low):
    rows = stack.shape[0] // 2
    both = jnp.dot(stack, right_high, preferred_element_type=F32)
    cross = jnp.dot(stack[:rows], right_low, preferred_element_type=F32)
    return both[:rows] + (both[rows:] + cross)


def kernel(
    na, nb, coef_ref, v_ref, a_ref, b_hbm, out_ref,
    strip, bt_high, bt_low, v_all, v_col, a_stack, a_col, square, u_all, total, stack,
    from_task, to_task,
    strip_sem, z_send, z_recv, a_send, a_recv, x_send, x_recv, v_send, v_recv,
    u_send, u_recv, m_send, m_recv, f_send, f_recv,
):
    a = lax.axis_index("alpha")
    b = lax.axis_index("beta")
    t = lax.axis_index("task")
    rows, cols = v_ref.shape
    full_a = a_ref.shape[1]
    half = cols // 2
    parts = half // TILE
    quarter = full_a // nb
    across = lax.rem(b + 2, 4)
    sibling = b + 1 - 2 * lax.rem(b, 2)
    diagonal = lax.rem(sibling + 2, 4)
    other = 1 - t

    barrier = pltpu.get_barrier_semaphore()
    for d in range(1, na):
        pl.semaphore_signal(barrier, inc=1, device_id={"alpha": lax.rem(a + d, na)}, device_id_type=MESH)
    pl.semaphore_signal(barrier, inc=1, device_id={"task": other}, device_id_type=MESH)
    pl.semaphore_signal(barrier, inc=1, device_id={"beta": across}, device_id_type=MESH)
    pl.semaphore_signal(barrier, inc=1, device_id={"beta": sibling}, device_id_type=MESH)
    pl.semaphore_wait(barrier, na + 2)

    def span(start, size):
        return pl.ds(pl.multiple_of(start, 128), size)

    def remote(src, dst, send, recv, where):
        return pltpu.make_async_remote_copy(
            src_ref=src, dst_ref=dst, send_sem=send, recv_sem=recv, device_id=where, device_id_type=MESH
        )

    def piece(side, q):
        return span(side * half + q * TILE, TILE)

    def rows_of(i):
        return pl.ds(pl.multiple_of(i * rows, 8), rows)

    def z_copy(q, d):
        return remote(
            v_ref.at[:, piece(t, q)], v_col.at[rows_of(a), piece(t, q)],
            z_send.at[q, d - 1], z_recv.at[q, d - 1], {"alpha": lax.rem(a + d, na)},
        )

    def x_copy(q, d):
        at = rows_of(lax.rem(a + na - d, na))
        return remote(
            v_col.at[at, piece(t, q)], v_col.at[at, piece(t, q)],
            x_send.at[q, d - 1], x_recv.at[q, d - 1], {"task": other},
        )

    def a_copy(d):
        return remote(
            a_ref.at[:, span(b * quarter, quarter)], a_col.at[rows_of(a), :],
            a_send.at[d - 1], a_recv.at[d - 1], {"alpha": lax.rem(a + d, na)},
        )

    def v_copy(n):
        return (
            lambda: remote(v_ref, v_all.at[b], v_send.at[0], v_recv.at[0], {"beta": across}),
            lambda: remote(v_ref, v_all.at[b], v_send.at[1], v_recv.at[1], {"beta": sibling}),
            lambda: remote(v_all.at[across], v_all.at[across], v_send.at[2], v_recv.at[2], {"beta": sibling}),
        )[n]()

    def u_copy(n, k, side, q):
        block = across if n == 2 else b
        ref = u_all.at[block, :, piece(side, q)]
        where = {"beta": across} if n == 0 else {"beta": sibling}
        return remote(ref, ref, u_send.at[n, k], u_recv.at[n, k], where)

    def m_copy(n):
        ref = square.at[:, span((across if n == 2 else b) * quarter, quarter)]
        where = {"beta": across} if n == 0 else {"beta": sibling}
        return remote(ref, ref, m_send.at[n], m_recv.at[n], where)

    def f_copy(q):
        at = pl.ds(q * TILE, TILE)
        return remote(to_task.at[:, at], from_task.at[:, at], f_send.at[q], f_recv.at[q], {"task": other})

    v_copy(0).start()
    v_copy(1).start()
    for q in range(parts):
        for d in range(1, na):
            z_copy(q, d).start()
    for d in range(1, na):
        a_copy(d).start()

    strips = cols // STRIP

    def strip_copy(r, slot):
        return pltpu.make_async_copy(
            b_hbm.at[pl.ds(pl.multiple_of(r * STRIP, STRIP), STRIP), :], strip.at[slot], strip_sem.at[slot]
        )

    strip_copy(0, 0).start()
    v_col[rows_of(a), :] = v_ref[...]
    a_col[rows_of(a), :] = a_ref[:, span(b * quarter, quarter)]
    a_stack[:rows, :], a_stack[rows:, :] = halves(a_ref[...])

    def take_strip(r, carry):
        slot = lax.rem(r, 2)

        @pl.when(r + 1 < strips)
        def _():
            strip_copy(r + 1, 1 - slot).start()

        strip_copy(r, slot).wait()

        def turn(n, inner):
            at = span(n * 512, 512)
            high, low = halves(strip[slot, :, at].T)
            bt_high[at, span(r * STRIP, STRIP)] = high
            bt_low[at, span(r * STRIP, STRIP)] = low
            return inner

        return lax.fori_loop(0, nb * cols // 512, turn, carry)

    lax.fori_loop(0, strips, take_strip, 0)

    def add_block(value, block, first):
        stack[:rows, :], stack[rows:, :] = halves(value)

        def column(n, carry):
            at = span(n * TILE, TILE)
            depth = span(block * cols, cols)
            term = product(stack[...], bt_high[depth, at], bt_low[depth, at])
            total[:, at] = term if first else total[:, at] + term
            return carry

        lax.fori_loop(0, cols // TILE, column, 0)

    def relay_v(q):
        for d in range(1, na):
            z_copy(q, d).wait_recv()
            x_copy(q, d).start()

    def make_u(k, side, q):
        at = piece(side, q)
        u_all[b, :, at] = total[:, at] + 2.0 * product(a_stack[...], *halves(v_col[:, at]))
        u_copy(0, k, side, q).start()
        u_copy(1, k, side, q).start()

    add_block(v_ref[...], b, True)
    v_copy(1).wait_recv()
    add_block(v_all[sibling], sibling, False)
    relay_v(0)
    v_copy(0).wait_recv()
    v_copy(2).start()
    add_block(v_all[across], across, False)
    v_copy(2).wait_recv()
    add_block(v_all[diagonal], diagonal, False)
    order = []
    for q in range(parts):
        if q > 0:
            relay_v(q)
        make_u(2 * q, t, q)
        for d in range(1, na):
            x_copy(q, d).wait_recv()
        make_u(2 * q + 1, other, q)
        order += [(2 * q, t, q), (2 * q + 1, other, q)]

    add_block(u_all[b], b, True)
    for piece_of in order:
        u_copy(1, *piece_of).wait_recv()
    add_block(u_all[sibling], sibling, False)
    for piece_of in order:
        u_copy(0, *piece_of).wait_recv()
        u_copy(2, *piece_of).start()
    for d in range(1, na):
        a_copy(d).wait_recv()
    square[:, span(b * quarter, quarter)] = product(a_stack[...], *halves(a_col[...]))
    m_copy(0).start()
    m_copy(1).start()
    add_block(u_all[across], across, False)
    for piece_of in order:
        u_copy(2, *piece_of).wait_recv()
    add_block(u_all[diagonal], diagonal, False)
    m_copy(0).wait_recv()
    m_copy(2).start()
    m_copy(1).wait_recv()
    m_copy(2).wait_recv()
    a_stack[:rows, :], a_stack[rows:, :] = halves(square[...])
    coef = coef_ref[0]
    for q in range(parts):
        at = piece(other, q)
        to_task[:, q * TILE:(q + 1) * TILE] = coef * (total[:, at] + product(a_stack[...], *halves(v_col[:, at])))
        f_copy(q).start()
    for q in range(parts):
        at = piece(t, q)
        total[:, at] = coef * (total[:, at] + product(a_stack[...], *halves(v_col[:, at])))
    for q in range(parts):
        f_copy(q).wait_recv()
        out_ref[:, q * TILE:(q + 1) * TILE] = total[:, piece(t, q)] + from_task[:, q * TILE:(q + 1) * TILE]

    for q in range(parts):
        f_copy(q).wait_send()
        for d in range(1, na):
            z_copy(q, d).wait_send()
            x_copy(q, d).wait_send()
    for d in range(1, na):
        a_copy(d).wait_send()
    for n in range(3):
        v_copy(n).wait_send()
        m_copy(n).wait_send()
        for piece_of in order:
            u_copy(n, *piece_of).wait_send()


def scratch(na, nb, rows, cols, full_a):
    quarter = full_a // nb
    parts = cols // 2 // TILE
    buffers = [
        pltpu.VMEM((2, STRIP, nb * cols), F32),
        pltpu.VMEM((nb * cols, cols), BF16),
        pltpu.VMEM((nb * cols, cols), BF16),
        pltpu.VMEM((nb, rows, cols), F32),
        pltpu.VMEM((full_a, cols), F32),
        pltpu.VMEM((2 * rows, full_a), BF16),
        pltpu.VMEM((full_a, quarter), F32),
        pltpu.VMEM((rows, full_a), F32),
        pltpu.VMEM((nb, rows, cols), F32),
        pltpu.VMEM((rows, cols), F32),
        pltpu.VMEM((2 * rows, cols), BF16),
        pltpu.VMEM((rows, cols // 2), F32),
        pltpu.VMEM((rows, cols // 2), F32),
    ]
    dma = pltpu.SemaphoreType.DMA
    counts = [
        (2,), (parts, na - 1), (parts, na - 1), (na - 1,), (na - 1,), (parts, na - 1), (parts, na - 1),
        (3,), (3,), (3, 2 * parts), (3, 2 * parts), (3,), (3,), (parts,), (parts,),
    ]
    return buffers, [dma(c) for c in counts]


def fused(mesh, coefficient, vector, alpha_rows, beta_rows):
    na, nb = mesh.shape["alpha"], mesh.shape["beta"]
    rows, cols = vector.shape
    buffers, semaphores = scratch(na, nb, rows, cols, alpha_rows.shape[1])
    vmem = pl.BlockSpec(memory_space=pltpu.VMEM)
    return pl.pallas_call(
        functools.partial(kernel, na, nb),
        out_shape=jax.ShapeDtypeStruct((rows, cols // 2), F32),
        in_specs=[pl.BlockSpec(memory_space=pltpu.SMEM), vmem, vmem, pl.BlockSpec(memory_space=pl.ANY)],
        out_specs=vmem,
        scratch_shapes=buffers + semaphores,
        compiler_params=pltpu.CompilerParams(
            collective_id=0, has_side_effects=True, vmem_limit_bytes=60 * 1024 * 1024
        ),
    )(coefficient.reshape(1), vector, alpha_rows, beta_rows)


def fits(mesh, vector, alpha_rows):
    na, nb, nt = mesh.shape["alpha"], mesh.shape["beta"], mesh.shape["task"]
    rows, cols = vector.shape
    full_a = alpha_rows.shape[1]
    if nb != 4 or nt != 2 or na < 2 or cols % (2 * TILE) or rows % 8 or full_a % (128 * nb):
        return False
    buffers, _ = scratch(na, nb, rows, cols, full_a)
    size = sum(buf.dtype.itemsize * functools.reduce(lambda x, y: x * y, buf.shape) for buf in buffers)
    size += 4 * (rows * cols + rows * full_a + rows * cols // 2)
    return size < VMEM_BUDGET


def collective(coefficient, vector, alpha_rows, beta_rows):
    high = lax.Precision.HIGH

    def dot(x, y):
        return jnp.dot(x, y, precision=high, preferred_element_type=F32)

    def apply_operator(block):
        left = dot(alpha_rows, lax.all_gather(block, "alpha", axis=0, tiled=True))
        return left + lax.psum_scatter(dot(block, beta_rows), "beta", scatter_dimension=1, tiled=True)

    second = apply_operator(apply_operator(vector))
    return lax.psum_scatter(coefficient * second, "task", scatter_dimension=1, tiled=True)


def on_device(
    mesh, vector, op_alpha, op_beta, op_weight, alpha_string, beta_string, alpha_energy, beta_energy
):
    task_index = lax.axis_index("task")
    coefficient = 0.5 * op_weight[task_index]
    if fits(mesh, vector, op_alpha[0]):
        summed = fused(mesh, coefficient, vector, op_alpha[0], op_beta[0])
    else:
        summed = collective(coefficient, vector, op_alpha[0], op_beta[0])
    width = summed.shape[1]
    column_start = task_index * width
    own_strings = lax.dynamic_slice_in_dim(beta_string, column_start, width, 0)
    own_vector = lax.dynamic_slice_in_dim(vector, column_start, width, 1)
    diag = alpha_energy[alpha_string][:, None] + beta_energy[own_strings][None, :]
    return summed + diag * own_vector


def solution(mesh):
    return jax.shard_map(
        functools.partial(on_device, mesh),
        mesh=mesh,
        in_specs=(
            P("alpha", "beta"),
            P("task", "alpha", None),
            P("task", "beta", None),
            P(),
            P("alpha"),
            P("beta"),
            P(),
            P(),
        ),
        out_specs=P("alpha", ("beta", "task")),
        check_vma=False,
    )
```

time: 219 us -> 114 us (0.52)
  the two profiles are of different devices: /device:TPU:0 before, /device:TPU:25 now
where the time goes in v1:
time: 114 us
  Pallas kernels  103 us (90%)
  local copies, waits for them, and re-layouts  6.68 us (6%)
  other arithmetic  3.43 us (3%)
    pallas_call x1, Pallas kernels, fused(): pl.pallas_call(functools.partial(kernel, na, nb), out_shape=jax.ShapeDtyp...  103 us
    gather x1, local copies, waits for them, and re-layouts, on_device(): beta_energy[own_strings][None, :]  3.14 us

profile of v1, /device:TPU:25, one launch (start us, length us, event | category | flops | bytes accessed | tf_op | source)
XLA Modules:
  0.0 113.9 jit_solution(987769535407164628)
XLA Ops:
  0.0 0.0 copy-start
  0.0 0.0 copy-start.1
  0.0 1.3 %dynamic_slice.9 = f32[1]{0:T(128)} dynamic-slice(f32[2]{0:T(128)} %param.11, s32[]{:T(128)S(6)} %select_n.13), dynamic_slice_sizes={1} | dynamic-slice | bytes 12 | tf_op jit(solution)/shard_map/dynamic_slice | solution.py:315
  2.0 0.7 compare_select_fusion.1
  2.7 0.8 compare_select_fusion
  3.5 0.0 copy-done
  3.5 3.1 %gather_fusion.1 = f32[512]{0:T(512)S(1)} fusion(f32[65536]{0:T(1024)S(1)} %copy-done, s32[1024]{0:T(1024)S(1)} %pad_clamp_fusion), kind=kCustom, calls=%fused_computation.1 | custom fusion | bytes 6144 | tf_op jit(solution)/shard_map/gather | solution.py:324
  6.6 2.2 %gather_fusion = f32[256]{0:T(256)S(1)} fusion(f32[65536]{0:T(1024)} %param.14, s32[1024]{0:T(1024)S(1)} %pad_clamp_fusion.1), kind=kCustom, calls=%fused_computation | custom fusion | bytes 3072 | tf_op jit(solution)/shard_map/gather | solution.py:324
  8.8 103.1 %shard_map.82 = f32[256,512]{1,0:T(8,128)} custom-call(f32[1]{0:T(128)S(6)} %mul_shard_map.4.coef_ref, f32[256,1024]{1,0:T(8,128)} %v_ref.1, f32[256,1024]{1,0:T(8,128)} %bitcast.3, f32[1024,4096]{1,0:T(8,128)} %bitcast.2), custom_call_target="tpu_custom_call" | custom-call | tf_op jit(solution)/shard_map/pallas_call | solution.py:273
  111.9 0.0 copy-done.1
  111.9 2.0 %multiply_add_fusion = f32[256,512]{1,0:T(8,128)} fusion(f32[256,512]{1,0:T(8,128)} %shard_map.82, f32[256,1024]{1,0:T(8,128)S(1)} %copy-done.1, s32[]{:T(128)S(6)} %select_n.15, f32[512]{0:T(512)S(1)} %gather_fusion.1, f32[256]{0:T(256)S(1)} %gather_fusion), kind=kLoop, calls=%fused_computation.2 | loop fusion | flops 393216 | bytes 1575940 | tf_op jit(solution)/shard_map/add | solution.py:325
  (2 shorter events, 0.0 us)
Async XLA Ops:
  0.0 3.5 %copy-start = (f32[65536]{0:T(1024)S(1)}, f32[65536]{0:T(1024)}, u32[]{:S(2)}) copy-start(f32[65536]{0:T(1024)} %param.15) | copy-start | bytes 786436
  0.0 111.9 %copy-start.1 = (f32[256,1024]{1,0:T(8,128)S(1)}, f32[256,1024]{1,0:T(8,128)}, u32[]{:S(2)}) copy-start(f32[256,1024]{1,0:T(8,128)} %v_ref.1) | copy-start | bytes 3145732

commit v2 on v1

--- a/solution.py
+++ b/solution.py
@@ -11,6 +11,7 @@
 F32 = jnp.float32
 BF16 = jnp.bfloat16
 TILE = 256
+PIECE = 128
 STRIP = 128
 VMEM_BUDGET = 56 * 1024 * 1024
 
@@ -27,12 +28,26 @@
     return both[:rows] + (both[rows:] + cross)
 
 
+def look_up(table, index):
+    turned = table.T
+    high, rest = halves(turned)
+    middle = rest
+    low = (turned - high.astype(F32) - middle.astype(F32)).astype(BF16)
+    shape = (table.shape[0], index.shape[1])
+    hot = jnp.where(lax.broadcasted_iota(jnp.int32, shape, 0) == index // 128, 1.0, 0.0).astype(BF16)
+    found = jnp.dot(high, hot, preferred_element_type=F32) + (
+        jnp.dot(middle, hot, preferred_element_type=F32) + jnp.dot(low, hot, preferred_element_type=F32)
+    )
+    lane = lax.broadcasted_iota(jnp.int32, found.shape, 0) == lax.rem(index, 128)
+    return jnp.sum(jnp.where(lane, found, 0.0), axis=0, keepdims=True)
+
+
 def kernel(
-    na, nb, coef_ref, v_ref, a_ref, b_hbm, out_ref,
-    strip, bt_high, bt_low, v_all, v_col, a_stack, a_col, square, u_all, total, stack,
-    from_task, to_task,
-    strip_sem, z_send, z_recv, a_send, a_recv, x_send, x_recv, v_send, v_recv,
-    u_send, u_recv, m_send, m_recv, f_send, f_recv,
+    na, nb, weight_ref, v_ref, a_ref, alpha_table, beta_table, alpha_index, beta_index, b_hbm, out_ref,
+    strip, bt_high, bt_low, v_all, v_col, a_stack, gram, gram_in, scatter, scatter_in,
+    square, u_all, total, stack, from_task, to_task, alpha_part, beta_part,
+    strip_sem, z_send, z_recv, g_send, g_recv, e_send, e_recv, s_send, s_recv, x_send, x_recv,
+    v_send, v_recv, u_send, u_recv, m_send, m_recv, f_send, f_recv,
 ):
     a = lax.axis_index("alpha")
     b = lax.axis_index("beta")
@@ -40,12 +55,14 @@
     rows, cols = v_ref.shape
     full_a = a_ref.shape[1]
     half = cols // 2
-    parts = half // TILE
+    parts = half // PIECE
     quarter = full_a // nb
+    eighth = quarter // 2
     across = lax.rem(b + 2, 4)
     sibling = b + 1 - 2 * lax.rem(b, 2)
     diagonal = lax.rem(sibling + 2, 4)
     other = 1 - t
+    coef = 0.5 * weight_ref[t]
 
     barrier = pltpu.get_barrier_semaphore()
     for d in range(1, na):
@@ -64,7 +81,7 @@
         )
 
     def piece(side, q):
-        return span(side * half + q * TILE, TILE)
+        return span(side * half + q * PIECE, PIECE)
 
     def rows_of(i):
         return pl.ds(pl.multiple_of(i * rows, 8), rows)
@@ -82,11 +99,16 @@
             x_send.at[q, d - 1], x_recv.at[q, d - 1], {"task": other},
         )
 
-    def a_copy(d):
-        return remote(
-            a_ref.at[:, span(b * quarter, quarter)], a_col.at[rows_of(a), :],
-            a_send.at[d - 1], a_recv.at[d - 1], {"alpha": lax.rem(a + d, na)},
-        )
+    def g_copy():
+        return remote(gram.at[other], gram_in, g_send, g_recv, {"task": other})
+
+    def e_copy(d):
+        to = lax.rem(a + d, na)
+        return remote(scatter.at[rows_of(to), :], scatter_in.at[d - 1], e_send.at[d - 1], e_recv.at[d - 1], {"alpha": to})
+
+    def s_copy():
+        ref = square.at[:, span(b * quarter + t * eighth, eighth)]
+        return remote(ref, ref, s_send, s_recv, {"task": other})
 
     def v_copy(n):
         return (
@@ -115,9 +137,6 @@
     for q in range(parts):
         for d in range(1, na):
             z_copy(q, d).start()
-    for d in range(1, na):
-        a_copy(d).start()
-
     strips = cols // STRIP
 
     def strip_copy(r, slot):
@@ -127,8 +146,16 @@
 
     strip_copy(0, 0).start()
     v_col[rows_of(a), :] = v_ref[...]
-    a_col[rows_of(a), :] = a_ref[:, span(b * quarter, quarter)]
+    gram_left, gram_low = halves(a_ref[...].T)
+    right_high, right_low = halves(coef * a_ref[:, span(b * quarter, quarter)])
+    outer = jnp.dot(gram_left, right_high, preferred_element_type=F32) + (
+        jnp.dot(gram_low, right_high, preferred_element_type=F32)
+        + jnp.dot(gram_left, right_low, preferred_element_type=F32)
+    )
+    gram[0] = outer[:, :eighth]
+    gram[1] = outer[:, eighth:]
     a_stack[:rows, :], a_stack[rows:, :] = halves(a_ref[...])
+    g_copy().start()
 
     def take_strip(r, carry):
         slot = lax.rem(r, 2)
@@ -150,17 +177,22 @@
 
     lax.fori_loop(0, strips, take_strip, 0)
 
-    def add_block(value, block, first):
+    def load_block(value):
         stack[:rows, :], stack[rows:, :] = halves(value)
 
+    def add_columns(block, first, start, size):
         def column(n, carry):
-            at = span(n * TILE, TILE)
+            at = span(start + n * TILE, TILE)
             depth = span(block * cols, cols)
             term = product(stack[...], bt_high[depth, at], bt_low[depth, at])
             total[:, at] = term if first else total[:, at] + term
             return carry
 
-        lax.fori_loop(0, cols // TILE, column, 0)
+        lax.fori_loop(0, size // TILE, column, 0)
+
+    def add_block(value, block, first):
+        load_block(value)
+        add_columns(block, first, 0, cols)
 
     def relay_v(q):
         for d in range(1, na):
@@ -174,64 +206,97 @@
         u_copy(1, k, side, q).start()
 
     add_block(v_ref[...], b, True)
+    g_copy().wait_recv()
+    scatter[...] = gram[t] + gram_in[...]
+    relay_v(0)
+    for d in range(1, na):
+        e_copy(d).start()
     v_copy(1).wait_recv()
     add_block(v_all[sibling], sibling, False)
-    relay_v(0)
+    beta_part[...] = look_up(beta_table[...], beta_index[:, span(t * half, half)])
+    alpha_row = look_up(alpha_table[...], alpha_index[...])
+    alpha_part[...] = jnp.broadcast_to(alpha_row, (128, rows)).T
+    relay_v(1)
     v_copy(0).wait_recv()
     v_copy(2).start()
     add_block(v_all[across], across, False)
     v_copy(2).wait_recv()
     add_block(v_all[diagonal], diagonal, False)
+
     order = []
-    for q in range(parts):
+
+    def make_next(side, q):
+        make_u(len(order), side, q)
+        order.append((len(order), side, q))
+
+    for q in range(parts + 1):
+        if 2 <= q < parts:
+            relay_v(q)
+        if q < parts:
+            make_next(t, q)
         if q > 0:
-            relay_v(q)
-        make_u(2 * q, t, q)
-        for d in range(1, na):
-            x_copy(q, d).wait_recv()
-        make_u(2 * q + 1, other, q)
-        order += [(2 * q, t, q), (2 * q + 1, other, q)]
-
+            for d in range(1, na):
+                x_copy(q - 1, d).wait_recv()
+            make_next(other, q - 1)
+
+    def relay_u(pieces):
+        for piece_of in pieces:
+            u_copy(0, *piece_of).wait_recv()
+            u_copy(2, *piece_of).start()
+
+    relay_u(order[:-2])
     add_block(u_all[b], b, True)
+    for d in range(1, na):
+        e_copy(d).wait_recv()
+    mine = scatter[rows_of(a), :]
+    for d in range(1, na):
+        mine = mine + scatter_in[d - 1]
+    square[:, span(b * quarter + t * eighth, eighth)] = mine
     for piece_of in order:
         u_copy(1, *piece_of).wait_recv()
+    s_copy().start()
+    relay_u(order[-2:])
     add_block(u_all[sibling], sibling, False)
-    for piece_of in order:
-        u_copy(0, *piece_of).wait_recv()
-        u_copy(2, *piece_of).start()
-    for d in range(1, na):
-        a_copy(d).wait_recv()
-    square[:, span(b * quarter, quarter)] = product(a_stack[...], *halves(a_col[...]))
+    s_copy().wait_recv()
     m_copy(0).start()
     m_copy(1).start()
     add_block(u_all[across], across, False)
     for piece_of in order:
         u_copy(2, *piece_of).wait_recv()
-    add_block(u_all[diagonal], diagonal, False)
+    load_block(u_all[diagonal])
+    for q in range(half // TILE):
+        at = span(other * half + q * TILE, TILE)
+        add_columns(diagonal, False, other * half + q * TILE, TILE)
+        to_task[:, q * TILE:(q + 1) * TILE] = coef * total[:, at]
+        f_copy(q).start()
+    add_columns(diagonal, False, t * half, half)
     m_copy(0).wait_recv()
     m_copy(2).start()
     m_copy(1).wait_recv()
     m_copy(2).wait_recv()
     a_stack[:rows, :], a_stack[rows:, :] = halves(square[...])
-    coef = coef_ref[0]
+    for q in range(half // TILE):
+        at = span(t * half + q * TILE, TILE)
+        local = pl.ds(q * TILE, TILE)
+        diag = alpha_part[:, :1] + beta_part[:, local]
+        total[:, at] = (
+            coef * total[:, at] + product(a_stack[...], *halves(v_col[:, at])) + diag * v_ref[:, at]
+        )
+    for q in range(half // TILE):
+        f_copy(q).wait_recv()
+        local = pl.ds(q * TILE, TILE)
+        out_ref[:, local] = total[:, span(t * half + q * TILE, TILE)] + from_task[:, local]
+
+    for q in range(half // TILE):
+        f_copy(q).wait_send()
     for q in range(parts):
-        at = piece(other, q)
-        to_task[:, q * TILE:(q + 1) * TILE] = coef * (total[:, at] + product(a_stack[...], *halves(v_col[:, at])))
-        f_copy(q).start()
-    for q in range(parts):
-        at = piece(t, q)
-        total[:, at] = coef * (total[:, at] + product(a_stack[...], *halves(v_col[:, at])))
-    for q in range(parts):
-        f_copy(q).wait_recv()
-        out_ref[:, q * TILE:(q + 1) * TILE] = total[:, piece(t, q)] + from_task[:, q * TILE:(q + 1) * TILE]
-
-    for q in range(parts):
-        f_copy(q).wait_send()
         for d in range(1, na):
             z_copy(q, d).wait_send()
             x_copy(q, d).wait_send()
+    g_copy().wait_send()
+    s_copy().wait_send()
     for d in range(1, na):
-        a_copy(d).wait_send()
+        e_copy(d).wait_send()
     for n in range(3):
         v_copy(n).wait_send()
         m_copy(n).wait_send()
@@ -241,7 +306,8 @@
 
 def scratch(na, nb, rows, cols, full_a):
     quarter = full_a // nb
-    parts = cols // 2 // TILE
+    eighth = quarter // 2
+    parts = cols // 2 // PIECE
     buffers = [
         pltpu.VMEM((2, STRIP, nb * cols), F32),
         pltpu.VMEM((nb * cols, cols), BF16),
@@ -249,23 +315,31 @@
         pltpu.VMEM((nb, rows, cols), F32),
         pltpu.VMEM((full_a, cols), F32),
         pltpu.VMEM((2 * rows, full_a), BF16),
-        pltpu.VMEM((full_a, quarter), F32),
+        pltpu.VMEM((2, full_a, eighth), F32),
+        pltpu.VMEM((full_a, eighth), F32),
+        pltpu.VMEM((full_a, eighth), F32),
+        pltpu.VMEM((na - 1, rows, eighth), F32),
         pltpu.VMEM((rows, full_a), F32),
         pltpu.VMEM((nb, rows, cols), F32),
         pltpu.VMEM((rows, cols), F32),
         pltpu.VMEM((2 * rows, cols), BF16),
         pltpu.VMEM((rows, cols // 2), F32),
         pltpu.VMEM((rows, cols // 2), F32),
+        pltpu.VMEM((rows, 128), F32),
+        pltpu.VMEM((1, cols // 2), F32),
     ]
     dma = pltpu.SemaphoreType.DMA
+    tiles = cols // 2 // TILE
     counts = [
-        (2,), (parts, na - 1), (parts, na - 1), (na - 1,), (na - 1,), (parts, na - 1), (parts, na - 1),
-        (3,), (3,), (3, 2 * parts), (3, 2 * parts), (3,), (3,), (parts,), (parts,),
+        (2,), (parts, na - 1), (parts, na - 1), (), (), (na - 1,), (na - 1,), (), (), (parts, na - 1), (parts, na - 1),
+        (3,), (3,), (3, 2 * parts), (3, 2 * parts), (3,), (3,), (tiles,), (tiles,),
     ]
-    return buffers, [dma(c) for c in counts]
-
-
-def fused(mesh, coefficient, vector, alpha_rows, beta_rows):
+    return buffers, [dma(c) if c else dma for c in counts]
+
+
+def fused(
+    mesh, op_weight, vector, alpha_rows, beta_rows, alpha_string, beta_string, alpha_energy, beta_energy
+):
     na, nb = mesh.shape["alpha"], mesh.shape["beta"]
     rows, cols = vector.shape
     buffers, semaphores = scratch(na, nb, rows, cols, alpha_rows.shape[1])
@@ -273,20 +347,25 @@
     return pl.pallas_call(
         functools.partial(kernel, na, nb),
         out_shape=jax.ShapeDtypeStruct((rows, cols // 2), F32),
-        in_specs=[pl.BlockSpec(memory_space=pltpu.SMEM), vmem, vmem, pl.BlockSpec(memory_space=pl.ANY)],
+        in_specs=[pl.BlockSpec(memory_space=pltpu.SMEM)] + [vmem] * 6 + [pl.BlockSpec(memory_space=pl.ANY)],
         out_specs=vmem,
         scratch_shapes=buffers + semaphores,
         compiler_params=pltpu.CompilerParams(
             collective_id=0, has_side_effects=True, vmem_limit_bytes=60 * 1024 * 1024
         ),
-    )(coefficient.reshape(1), vector, alpha_rows, beta_rows)
-
-
-def fits(mesh, vector, alpha_rows):
+    )(
+        op_weight, vector, alpha_rows, alpha_energy.reshape(-1, 128), beta_energy.reshape(-1, 128),
+        alpha_string.reshape(1, -1), beta_string.reshape(1, -1), beta_rows,
+    )
+
+
+def fits(mesh, vector, alpha_rows, alpha_energy, beta_energy):
     na, nb, nt = mesh.shape["alpha"], mesh.shape["beta"], mesh.shape["task"]
     rows, cols = vector.shape
     full_a = alpha_rows.shape[1]
-    if nb != 4 or nt != 2 or na < 2 or cols % (2 * TILE) or rows % 8 or full_a % (128 * nb):
+    if nb != 4 or nt != 2 or na < 2 or cols % (2 * TILE) or rows % 128 or full_a % (256 * nb):
+        return False
+    if cols // 2 < 2 * PIECE or alpha_energy.size % 128 or beta_energy.size % 128:
         return False
     buffers, _ = scratch(na, nb, rows, cols, full_a)
     size = sum(buf.dtype.itemsize * functools.reduce(lambda x, y: x * y, buf.shape) for buf in buffers)
@@ -311,12 +390,13 @@
 def on_device(
     mesh, vector, op_alpha, op_beta, op_weight, alpha_string, beta_string, alpha_energy, beta_energy
 ):
+    if fits(mesh, vector, op_alpha[0], alpha_energy, beta_energy):
+        return fused(
+            mesh, op_weight, vector, op_alpha[0], op_beta[0],
+            alpha_string, beta_string, alpha_energy, beta_energy,
+        )
     task_index = lax.axis_index("task")
-    coefficient = 0.5 * op_weight[task_index]
-    if fits(mesh, vector, op_alpha[0]):
-        summed = fused(mesh, coefficient, vector, op_alpha[0], op_beta[0])
-    else:
-        summed = collective(coefficient, vector, op_alpha[0], op_beta[0])
+    summed = collective(0.5 * op_weight[task_index], vector, op_alpha[0], op_beta[0])
     width = summed.shape[1]
     column_start = task_index * width
     own_strings = lax.dynamic_slice_in_dim(beta_string, column_start, width, 0)

time: 114 us -> 95 us (0.83)
  the two profiles are of different devices: /device:TPU:25 before, /device:TPU:8 now
where the time goes in v2:
time: 95 us; the launch traced here: 94.6 us
  Pallas kernels  92.8 us (98%)
  local copies, waits for them, and re-layouts  1.87 us (2%)
    pallas_call x1, Pallas kernels, fused(): pl.pallas_call(functools.partial(kernel, na, nb), out_shape=jax.ShapeDtyp...  92.8 us

profile of v2, /device:TPU:8, one launch (start us, length us, event | category | flops | bytes accessed | tf_op | source)
XLA Modules:
  0.0 94.6 jit_solution(9952044956139072288)
XLA Ops:
  0.0 92.8 %shard_map.82 = f32[256,512]{1,0:T(8,128)} custom-call(f32[2]{0:T(128)} %weight_ref.1, f32[256,1024]{1,0:T(8,128)} %v_ref.1, f32[256,1024]{1,0:T(8,128)} %bitcast.7, f32[512,128]{1,0:T(8,128)} %bitcast.8, f32[512,128]{1,0:T(8,128)} %bitcast.9, s32[1,256]{1,0:T(1,128)} %bitcast.11, s32[1,1024]{1,0:T(1,128)} %bitcast.10, f32[1024,4096]{1,0:T(8,128)} %bitcast.6), custom_call_target="tpu_custom_call" | custom-call | tf_op jit(solution)/shard_map/pallas_call | solution.py:347
  92.8 1.9 %copy.10 = f32[256,512]{1,0:T(8,128)} copy(f32[256,512]{1,0:T(8,128)} %shard_map.82) | data formatting | bytes 1048576

commit v3 on v2

--- a/solution.py
+++ b/solution.py
@@ -46,7 +46,7 @@
     na, nb, weight_ref, v_ref, a_ref, alpha_table, beta_table, alpha_index, beta_index, b_hbm, out_ref,
     strip, bt_high, bt_low, v_all, v_col, a_stack, gram, gram_in, scatter, scatter_in,
     square, u_all, total, stack, from_task, to_task, alpha_part, beta_part,
-    strip_sem, z_send, z_recv, g_send, g_recv, e_send, e_recv, s_send, s_recv, x_send, x_recv,
+    strip_sem, z_send, z_recv, r_send, g_send, g_recv, e_send, e_recv, s_send, s_recv, x_send, x_recv,
     v_send, v_recv, u_send, u_recv, m_send, m_recv, f_send, f_recv,
 ):
     a = lax.axis_index("alpha")
@@ -63,6 +63,10 @@
     diagonal = lax.rem(sibling + 2, 4)
     other = 1 - t
     coef = 0.5 * weight_ref[t]
+    inner = lax.rem(a + 1, 4) >= 2
+
+    def peer(d):
+        return (a, a + 1 - 2 * lax.rem(a, 2), lax.rem(a + 2, 4), 3 - a)[d]
 
     barrier = pltpu.get_barrier_semaphore()
     for d in range(1, na):
@@ -89,11 +93,15 @@
     def z_copy(q, d):
         return remote(
             v_ref.at[:, piece(t, q)], v_col.at[rows_of(a), piece(t, q)],
-            z_send.at[q, d - 1], z_recv.at[q, d - 1], {"alpha": lax.rem(a + d, na)},
-        )
+            z_send.at[q, d - 1], z_recv.at[q, d - 1], {"alpha": peer(d)},
+        )
+
+    def z_relay(q):
+        ref = v_col.at[rows_of(peer(2)), piece(t, q)]
+        return remote(ref, ref, r_send.at[q], z_recv.at[q, 2], {"alpha": peer(1)})
 
     def x_copy(q, d):
-        at = rows_of(lax.rem(a + na - d, na))
+        at = rows_of(peer(d))
         return remote(
             v_col.at[at, piece(t, q)], v_col.at[at, piece(t, q)],
             x_send.at[q, d - 1], x_recv.at[q, d - 1], {"task": other},
@@ -103,7 +111,7 @@
         return remote(gram.at[other], gram_in, g_send, g_recv, {"task": other})
 
     def e_copy(d):
-        to = lax.rem(a + d, na)
+        to = peer(d)
         return remote(scatter.at[rows_of(to), :], scatter_in.at[d - 1], e_send.at[d - 1], e_recv.at[d - 1], {"alpha": to})
 
     def s_copy():
@@ -135,8 +143,12 @@
     v_copy(0).start()
     v_copy(1).start()
     for q in range(parts):
-        for d in range(1, na):
-            z_copy(q, d).start()
+        z_copy(q, 1).start()
+        z_copy(q, 2).start()
+
+        @pl.when(inner)
+        def _():
+            z_copy(q, 3).start()
     strips = cols // STRIP
 
     def strip_copy(r, slot):
@@ -195,7 +207,14 @@
         add_columns(block, first, 0, cols)
 
     def relay_v(q):
-        for d in range(1, na):
+        z_copy(q, 2).wait_recv()
+
+        @pl.when(inner)
+        def _():
+            z_relay(q).start()
+
+        x_copy(q, 2).start()
+        for d in (1, 3):
             z_copy(q, d).wait_recv()
             x_copy(q, d).start()
 
@@ -256,11 +275,13 @@
         u_copy(1, *piece_of).wait_recv()
     s_copy().start()
     relay_u(order[-2:])
-    add_block(u_all[sibling], sibling, False)
+    load_block(u_all[sibling])
+    add_columns(sibling, False, other * half, half)
     s_copy().wait_recv()
     m_copy(0).start()
     m_copy(1).start()
-    add_block(u_all[across], across, False)
+    load_block(u_all[across])
+    add_columns(across, False, other * half, half)
     for piece_of in order:
         u_copy(2, *piece_of).wait_recv()
     load_block(u_all[diagonal])
@@ -269,7 +290,14 @@
         add_columns(diagonal, False, other * half + q * TILE, TILE)
         to_task[:, q * TILE:(q + 1) * TILE] = coef * total[:, at]
         f_copy(q).start()
-    add_columns(diagonal, False, t * half, half)
+
+    def own_half(n, carry):
+        block = lax.rem(b + n, nb)
+        load_block(u_all[block])
+        add_columns(block, False, t * half, half)
+        return carry
+
+    lax.fori_loop(1, nb, own_half, 0)
     m_copy(0).wait_recv()
     m_copy(2).start()
     m_copy(1).wait_recv()
@@ -290,8 +318,15 @@
     for q in range(half // TILE):
         f_copy(q).wait_send()
     for q in range(parts):
+        z_copy(q, 1).wait_send()
+        z_copy(q, 2).wait_send()
+
+        @pl.when(inner)
+        def _():
+            z_copy(q, 3).wait_send()
+            z_relay(q).wait_send()
+
         for d in range(1, na):
-            z_copy(q, d).wait_send()
             x_copy(q, d).wait_send()
     g_copy().wait_send()
     s_copy().wait_send()
@@ -331,7 +366,7 @@
     dma = pltpu.SemaphoreType.DMA
     tiles = cols // 2 // TILE
     counts = [
-        (2,), (parts, na - 1), (parts, na - 1), (), (), (na - 1,), (na - 1,), (), (), (parts, na - 1), (parts, na - 1),
+        (2,), (parts, na - 1), (parts, na - 1), (parts,), (), (), (na - 1,), (na - 1,), (), (), (parts, na - 1), (parts, na - 1),
         (3,), (3,), (3, 2 * parts), (3, 2 * parts), (3,), (3,), (tiles,), (tiles,),
     ]
     return buffers, [dma(c) if c else dma for c in counts]
@@ -363,7 +398,7 @@
     na, nb, nt = mesh.shape["alpha"], mesh.shape["beta"], mesh.shape["task"]
     rows, cols = vector.shape
     full_a = alpha_rows.shape[1]
-    if nb != 4 or nt != 2 or na < 2 or cols % (2 * TILE) or rows % 128 or full_a % (256 * nb):
+    if nb != 4 or nt != 2 or na != 4 or cols % (2 * TILE) or rows % 128 or full_a % (256 * nb):
         return False
     if cols // 2 < 2 * PIECE or alpha_energy.size % 128 or beta_energy.size % 128:
         return False

time: 95 us -> 88.7 us (0.934)
  the two profiles are of different devices: /device:TPU:8 before, /device:TPU:0 now
where the time goes in v3:
time: 88.7 us; the launch traced here: 88.3 us
  Pallas kernels  86.4 us (97%)
  local copies, waits for them, and re-layouts  1.87 us (2%)
    pallas_call x1, Pallas kernels, fused(): pl.pallas_call(functools.partial(kernel, na, nb), out_shape=jax.ShapeDtyp...  86.4 us
    unnamed x1, local copies, waits for them, and re-layouts  1.87 us

profile of v3, /device:TPU:0, one launch (start us, length us, event | category | flops | bytes accessed | tf_op | source)
XLA Modules:
  0.0 88.3 jit_solution(17337394110257347521)
XLA Ops:
  0.0 86.4 %shard_map.82 = f32[256,512]{1,0:T(8,128)} custom-call(f32[2]{0:T(128)} %weight_ref.1, f32[256,1024]{1,0:T(8,128)} %v_ref.1, f32[256,1024]{1,0:T(8,128)} %bitcast.7, f32[512,128]{1,0:T(8,128)} %bitcast.8, f32[512,128]{1,0:T(8,128)} %bitcast.9, s32[1,256]{1,0:T(1,128)} %bitcast.11, s32[1,1024]{1,0:T(1,128)} %bitcast.10, f32[1024,4096]{1,0:T(8,128)} %bitcast.6), custom_call_target="tpu_custom_call" | custom-call | tf_op jit(solution)/shard_map/pallas_call | solution.py:382
  86.4 1.9 %copy.10 = f32[256,512]{1,0:T(8,128)} copy(f32[256,512]{1,0:T(8,128)} %shard_map.82) | data formatting | bytes 1048576
